TPU v7x, 128 devices: a whole 4x4x4 slice. The times are simulated.
128 devices in a mesh: blk: 32 (over x, y, core), mp: 4 (over z).
Axes of the slice: x: 4, y: 4, z: 4, core: 2. Of those that a mesh axis runs over, the one named last changes fastest.
Arguments:
- hidden: bfloat16 [144, 3584], replicated, may hold values from -6 to 6
- medusa_w: bfloat16 [2, 3584, 3584], P(None, 'blk', 'mp'), may hold values from -0.09375 to 0.09375
- embedding: bfloat16 [131072, 3584], P(('blk', 'mp')), may hold values from -0.5 to 0.5
- cand_ids: int32 [2, 144, 10], replicated, may hold values from 0 to 131071
- tree_q: bfloat16 [12, 48, 4096], P(None, None, 'mp'), may hold values from -6 to 6
- tree_key_value: bfloat16 [2, 12, 48, 2048], P(None, None, None, 'mp'), may hold values from -6 to 6
- prompt_key_value: bfloat16 [2, 32, 2048, 2048], P(None, 'blk', None, 'mp'), may hold values from -6 to 6
- block_group: int32 [32], P('blk'), may hold values from 0 to 11, as said below
- block_len: int32 [32], P('blk'), may hold values from 1 to 2048
- block_empty: int32 [32], P('blk'), may hold values 0 or 1
- parents: int32 [12, 48], replicated, may hold values from 0 to 46, as said below
- out_weight: bfloat16 [4096, 3584], P('mp'), may hold values from -0.09375 to 0.09375
- post_gain: float32 [3584], replicated, may hold values from 0.5 to 1.5
- resid: bfloat16 [576, 3584], P('blk'), may hold values from -6 to 6
Outputs:
- draft_logprob: float32 [2, 144, 10], replicated
- layer_out: bfloat16 [576, 3584], P('blk')
Inputs may be any that keep to these rules, and one draw needn't show every extreme that they name: `block_group`: every group number from 0 to min(12, 32) - 1 owns at least one block. `parents`: entry 0 of each row is 0; entry i for i >= 1 is below i; some group's last token has parent 48 - 2.
All inputs are finite; a program needn't handle non-finite values. No bound on the sum of `block_empty` on one device may be relied on, other than what follows from the above.
Results may differ from a plain program's by a relative error of at most 0.005.
Values may be sent and summed in bfloat16 or wider, within the bound.
A program may use at most 128 MiB of HBM per device.

v0:
```python
import jax
import jax.numpy as jnp
from jax import lax
from jax.sharding import PartitionSpec as P

HEAD_SIZE = 256


def capped(values, limit):
    return limit * jnp.tanh(values / limit)


def ancestry(parents):
    count = parents.shape[1]
    column = jnp.arange(count, dtype=jnp.int32)
    linked = (parents[:, :, None] == column[None, None, :]) & (column[None, :, None] > 0)
    reach = jnp.eye(count, dtype=jnp.float32)[None] + linked.astype(jnp.float32)
    for sweep in range(count.bit_length()):
        reach = jnp.minimum(
            jnp.einsum("gij,gjk->gik", reach, reach, precision=lax.Precision.HIGHEST), 1.0
        )
    return reach


def attend(queries, keys, values, mask):
    rows = queries.shape[0]
    length = keys.shape[0]
    kv_heads = keys.shape[1] // HEAD_SIZE
    repeats = queries.shape[1] // keys.shape[1]
    query_view = queries.reshape(rows, kv_heads, repeats, HEAD_SIZE)
    key_view = keys.reshape(length, kv_heads, HEAD_SIZE)
    value_view = values.reshape(length, kv_heads, HEAD_SIZE)
    scores = jnp.einsum(
        "qhrd,khd->hrqk", query_view, key_view, preferred_element_type=jnp.float32
    ) * HEAD_SIZE ** (-0.5)
    weights = jnp.exp(capped(scores, 50.0)) * mask[None, None]
    denominator = jnp.sum(weights, -1).transpose(2, 0, 1).reshape(rows, kv_heads * repeats)
    numerator = jnp.einsum(
        "hrqk,khd->qhrd",
        weights.astype(jnp.bfloat16),
        value_view,
        preferred_element_type=jnp.float32,
    )
    return (numerator.reshape(rows, kv_heads * repeats * HEAD_SIZE), denominator)


def per_device(
    hidden,
    medusa_w,
    embedding,
    cand_ids,
    tree_q,
    tree_key_value,
    prompt_key_value,
    block_group,
    block_len,
    block_empty,
    parents,
    out_weight,
    post_gain,
    resid,
):
    units = medusa_w.shape[2]
    inner = jnp.einsum(
        "rd,mdu->mru",
        hidden,
        lax.all_gather(medusa_w, "blk", axis=1, tiled=True),
        preferred_element_type=jnp.float32,
    )
    own_cols = lax.dynamic_slice_in_dim(hidden, lax.axis_index("mp") * units, units, 1).astype(
        jnp.float32
    )
    fresh = (own_cols[None] + jax.nn.silu(inner)).astype(jnp.bfloat16)
    full_fresh = lax.all_gather(fresh, "mp", axis=2, tiled=True)
    logits = capped(
        jnp.einsum("mrd,vd->mrv", full_fresh, embedding, preferred_element_type=jnp.float32), 30.0
    )
    totals = jnp.sum(jnp.exp(logits), -1)
    vocab_dev = embedding.shape[0]
    first_id = lax.axis_index(("blk", "mp")) * vocab_dev
    local_ids = cand_ids - first_id
    match = local_ids[..., None] == jnp.arange(vocab_dev, dtype=jnp.int32)
    picked = jnp.sum(jnp.where(match, logits[:, :, None, :], 0.0), -1)
    totals, picked = lax.psum((totals, picked), ("blk", "mp"))
    draft_logprob = picked - jnp.log(totals)[..., None]
    groups, tree_size, features = tree_q.shape
    keys = prompt_key_value[0, 0]
    values = prompt_key_value[1, 0]
    length = keys.shape[0]
    group = block_group[0]
    key_ok = ((jnp.arange(length, dtype=jnp.int32) < block_len[0]) & (block_empty[0] == 0)).astype(
        jnp.float32
    )
    row_group = jnp.arange(groups * tree_size, dtype=jnp.int32) // tree_size
    mask = (row_group == group).astype(jnp.float32)[:, None] * key_ok[None, :]
    numer, denom = attend(tree_q.reshape(groups * tree_size, features), keys, values, mask)
    rows_dev = groups * tree_size // lax.axis_size("blk")
    first_row = lax.axis_index("blk") * rows_dev
    summed = lax.psum((numer, denom), "blk")
    numer = lax.dynamic_slice_in_dim(summed[0], first_row, rows_dev, 0)
    denom = lax.dynamic_slice_in_dim(summed[1], first_row, rows_dev, 0)
    reach = ancestry(parents)
    tree_numer, tree_denom = jax.vmap(attend)(tree_q, tree_key_value[0], tree_key_value[1], reach)
    heads_dev = tree_denom.shape[2]
    tree_numer = lax.dynamic_slice_in_dim(
        tree_numer.reshape(groups * tree_size, features), first_row, rows_dev, 0
    )
    tree_denom = lax.dynamic_slice_in_dim(
        tree_denom.reshape(groups * tree_size, heads_dev), first_row, rows_dev, 0
    )
    numer = numer + tree_numer
    denom = denom + tree_denom
    heads_out = (
        (numer.reshape(rows_dev, heads_dev, HEAD_SIZE) / denom[..., None])
        .reshape(rows_dev, features)
        .astype(jnp.bfloat16)
    )
    attn = lax.psum(jnp.dot(heads_out, out_weight, preferred_element_type=jnp.float32), "mp")
    normed = attn * lax.rsqrt(jnp.mean(attn * attn, -1, keepdims=True) + 1e-06) * post_gain
    layer_out = (normed + resid.astype(jnp.float32)).astype(jnp.bfloat16)
    return (draft_logprob, layer_out)


def solution(mesh):
    placed = (
        P(),
        P(None, "blk", "mp"),
        P(("blk", "mp"), None),
        P(),
        P(None, None, "mp"),
        P(None, None, None, "mp"),
        P(None, "blk", None, "mp"),
        P("blk"),
        P("blk"),
        P("blk"),
        P(),
        P("mp", None),
        P(),
        P("blk", None),
    )
    return jax.shard_map(
        per_device, mesh=mesh, in_specs=placed, out_specs=(P(), P("blk", None)), check_vma=False
    )
```

profile of v0, /device:TPU:1, one launch (start us, length us, event | category | flops | bytes accessed | tf_op | source)
XLA Modules:
  0.0 381.7 jit_solution(4261685247920140671)
XLA Ops:
  7.2 4.4 %fusion.51 = (bf16[1,1,2048,512]{3,2,1,0:T(8,128)(2,1)}, bf16[1,1,2048,512]{3,2,1,0:T(8,128)(2,1)}) fusion(bf16[2,1,2048,512]{3,2,1,0:T(8,128)(2,1)} %param.20), kind=kLoop, calls=%fused_computation.70 | loop fusion | bytes 8388608 | tf_op jit(solution)/shard_map/slice | solution.py:88
  11.6 2.9 copy.79
  16.5 3.3 reshape_reshape.3
  19.8 4.0 %copy.80 = bf16[1,1,2048,512]{2,3,1,0:T(8,128)(2,1)} copy(bf16[1,1,2048,512]{3,2,1,0:T(8,128)(2,1)} %get-tuple-element.6) | data formatting | bytes 4194304
  24.2 10.5 %fusion = (f32[2,2,576]{2,1,0:T(2,128)}, f32[2,2048,576,2]{1,2,3,0:T(8,128)}) fusion(f32[576,2048]{1,0:T(8,128)S(1)} %broadcast_multiply_fusion, bf16[2048,2,256,1]{0,2,3,1:T(8,128)(2,1)S(1)} %bitcast.83, bf16[576,2,2,256]{3,2,1,0:T(2,128)(2,1)S(1)} %reshape_reshape.3), kind=kOutput, calls=%fused_computation.1 | convolution fusion | flops 2434791168 | bytes 26878976 | tf_op jit(solution)/shard_map/qhrd,khd->hrqk/dot_general | solution.py:33
  34.7 9.1 %fusion.6 = f32[576,2,2,256]{3,0,2,1:T(8,128)S(1)} fusion(bf16[2048,2,256,1]{0,2,3,1:T(8,128)(2,1)S(1)} %bitcast.85, f32[2,2048,576,2]{1,2,3,0:T(8,128)} %get-tuple-element.15, f32[576,2048]{1,0:T(8,128)S(1)} %broadcast_multiply_fusion), kind=kOutput, calls=%fused_computation.10 | convolution fusion | flops 2434793472 | bytes 28049408 | tf_op jit(solution)/shard_map/hrqk,khd->qhrd/dot_general | solution.py:38
  43.8 1.8 copy.56
  45.6 2.9 reshape.101
  48.6 0.7 all-gather.3.cloned.1.call-update
  49.8 0.9 reshape.102
  50.7 0.7 reshape.104
  51.7 1.4 convolution_minimum_fusion.5
  53.5 0.4 convolution_minimum_fusion.3
  53.9 0.4 convolution_minimum_fusion.2
  54.4 0.4 convolution_minimum_fusion.1
  54.8 0.4 convolution_minimum_fusion
  55.3 0.9 fusion.53
  56.3 124.9 %psum.38 = f32[576,4]{0,1:T(4,128)S(1)} all-reduce(f32[576,4]{0,1:T(4,128)S(1)} %reshape.104), channel_id=1, replica_groups=mesh['blk'=32,'mp'=4] {'blk'}, use_global_device_ids=true, to_apply=%region_6.7 | all-reduce | flops 2304 | bytes 18432 | tf_op jit(solution)/shard_map/psum | solution.py:99
  181.7 0.5 convolution_bitcast_fusion
  182.2 1.8 copy.62
  184.1 2.9 reshape.103
  187.1 5.1 %fusion.39 = f32[18,3584]{1,0:T(8,128)} fusion(bf16[1024,3584]{1,0:T(8,128)(2,1)} %param.25, f32[18,1024]{1,0:T(8,128)S(1)} %bitcast.87, f32[576,1024]{1,0:T(8,128)} %reshape.103, s32[]{:T(128)S(6)} %select_n.25, f32[576,1024]{1,0:T(8,128)} %all-reduce.4.cloned.1.call-done), kind=kOutput, calls=%fused_computation.47 | convolution fusion | flops 132175872 | bytes 7868420 | tf_op jit(solution)/shard_map/dot_general | solution.py:118
  192.4 32.7 %all-gather.3.cloned.1.call-done = bf16[2,3584,896]{2,1,0:T(8,128)(2,1)} async-done(((bf16[2,112,896]{2,1,0:T(8,128)(2,1)}), bf16[2,3584,896]{2,1,0:T(8,128)(2,1)}) %all-gather.3.cloned.1.call-update) | async-done | bytes 12845072 | tf_op jit(solution)/shard_map/all_gather | solution.py:67
  225.2 7.6 %add_convert_fusion = bf16[2,144,896]{2,1,0:T(8,128)(2,1)} fusion(bf16[2,3584,896]{2,1,0:T(8,128)(2,1)} %all-gather.3.cloned.1.call-done, bf16[144,3584]{1,0:T(8,128)(2,1)S(1)} %copy-done.4, f32[144,896]{1,0:T(8,128)S(1)} %dynamic-slice_convert_fusion), kind=kOutput, calls=%fused_computation.32 | convolution fusion | flops 1851236352 | bytes 14909440 | tf_op jit(solution)/shard_map/rd,mdu->mru/dot_general | solution.py:64
  232.8 34.1 %all-reduce.6.cloned.1.call-done = f32[18,3584]{1,0:T(8,128)} async-done(((f32[18,3584]{1,0:T(8,128)}), f32[18,3584]{1,0:T(8,128)}) %all-reduce.6.cloned.1.call-update) | async-done | bytes 258064 | tf_op jit(solution)/shard_map/psum | solution.py:118
  266.9 1.1 multiply_reduce_fusion
  268.0 1.8 add_convert_fusion.1
  269.8 31.7 %all-gather.5.cloned.1.call-done = bf16[2,144,3584]{2,1,0:T(8,128)(2,1)} async-done(((bf16[2,144,896]{2,1,0:T(8,128)(2,1)}), bf16[2,144,3584]{2,1,0:T(8,128)(2,1)}) %all-gather.5.cloned.1.call-update) | async-done | bytes 2064400 | tf_op jit(solution)/shard_map/all_gather | solution.py:74
  301.5 6.2 %exponential_reduce_fusion = (f32[2,144]{1,0:T(2,128)S(1)}, f32[2,144,1024]{2,1,0:T(8,128)S(1)}) fusion(bf16[2,144,3584]{2,1,0:T(8,128)(2,1)} %all-gather.5.cloned.1.call-done, bf16[1024,3584]{1,0:T(8,128)(2,1)} %param.16), kind=kOutput, calls=%fused_computation.24 | convolution fusion | flops 2114813696 | bytes 10585216 | tf_op jit(solution)/shard_map/mrd,vd->mrv/dot_general | solution.py:76
  307.8 1.8 select_reduce_fusion
  309.6 64.9 %all-reduce = (f32[2,144,10]{1,2,0:T(8,128)S(1)}, f32[2,144]{1,0:T(2,128)S(1)}) all-reduce(f32[2,144,10]{1,2,0:T(8,128)S(1)} %select_reduce_fusion, f32[2,144]{1,0:T(2,128)S(1)} %get-tuple-element.10), channel_id=1, replica_groups=mesh['blk'=32,'mp'=4] {'blk','mp'}, use_global_device_ids=true, to_apply=%region_1.2 | all-reduce | flops 3168 | bytes 25344 | tf_op jit(solution)/shard_map/psum | solution.py:84
  374.5 0.6 copy.65
  (45 shorter events, 2.7 us)
Async XLA Ops:
  7.2 179.9 %all-reduce.4.cloned.1.call-start = ((), (), s32[]{:S(2)}) async-start(), calls=%async_computation.2 | async-start | bytes 4718592 | tf_op jit(solution)/shard_map/psum | solution.py:99
  24.2 10.5 %copy-start.1 = (bf16[1,1,2048,512]{2,3,1,0:T(8,128)(2,1)S(1)}, bf16[1,1,2048,512]{2,3,1,0:T(8,128)(2,1)}, u32[]{:S(2)}) copy-start(bf16[1,1,2048,512]{2,3,1,0:T(8,128)(2,1)} %copy.80) | copy-start | bytes 6291460
  48.6 1.3 copy-start
  48.6 2.9 copy-start.2
  48.6 176.6 %all-gather.3.cloned.1.call-start = ((), (), s32[]{:S(2)}) async-start(), calls=%async_computation | async-start | bytes 13246464 | tf_op jit(solution)/shard_map/all_gather | solution.py:67
  49.3 217.6 %all-reduce.6.cloned.1.call-start = ((), (), s32[]{:S(2)}) async-start(), calls=%async_computation.3 | async-start | bytes 688128 | tf_op jit(solution)/shard_map/psum | solution.py:118
  184.0 3.0 copy-start.4
  192.1 40.7 %copy-start.5 = (s32[2,144,10]{1,0,2:T(2,128)S(1)}, s32[2,144,10]{1,0,2:T(2,128)}, u32[]{:S(2)}) copy-start(s32[2,144,10]{1,0,2:T(2,128)} %param.17) | copy-start | bytes 34564
  192.2 75.9 %copy-start.3 = (bf16[18,3584]{1,0:T(8,128)(2,1)S(1)}, bf16[18,3584]{1,0:T(8,128)(2,1)}, u32[]{:S(2)}) copy-start(bf16[18,3584]{1,0:T(8,128)(2,1)} %param.27) | copy-start | bytes 387076
  192.2 75.9 %copy-start.6 = (f32[3584]{0:T(1024)S(1)}, f32[3584]{0:T(1024)}, u32[]{:S(2)}) copy-start(f32[3584]{0:T(1024)} %param.26) | copy-start | bytes 43012
  192.2 109.4 %all-gather.5.cloned.1.call-start = ((), (), s32[]{:S(2)}) async-start(), calls=%async_computation.1 | async-start | bytes 2580480 | tf_op jit(solution)/shard_map/all_gather | solution.py:74
Sparse Core Ops, SparseCore 0:
  48.7 110.4 all-reduce.3
  161.6 63.5 all-gather.2
  227.5 39.3 all-reduce.5
  268.4 33.0 all-gather.4
where the time goes:
time: 382 us
  blocking collectives  190 us (50%)
  waiting for transfers between devices  99.3 us (26%)
  matrix products  43.3 us (11%)
  local copies, waits for them, and re-layouts  27.5 us (7%)
  between operations  16 us (4%)
  other arithmetic  5.25 us (1%)
    psum x1, blocking collectives, per_device(): summed = lax.psum((numer, denom), 'blk')  125 us
    psum x1, blocking collectives, per_device(): totals, picked = lax.psum((totals, picked), ('blk', 'mp'))  64.9 us
    psum x1, waiting for transfers between devices, per_device(): lax.psum(jnp.dot(heads_out, out_weight, preferred_element_type=jnp.float3...  34.1 us
    all_gather x1, waiting for transfers between devices, per_device(): lax.all_gather(medusa_w, 'blk', axis=1, tiled=True)  32.7 us
    all_gather x1, waiting for transfers between devices, per_device(): full_fresh = lax.all_gather(fresh, 'mp', axis=2, tiled=True)  31.7 us
    dot_general x2, matrix products, attend(): jnp.einsum('qhrd,khd->hrqk', query_view, key_view, preferred_element_type...  11.3 us
    dot_general x2, matrix products, attend(): jnp.einsum('hrqk,khd->qhrd', weights.astype(jnp.bfloat16), value_view, pr...  9.63 us
    unnamed x19, local copies, waits for them, and re-layouts  7.84 us
  transfers between devices with their start and end apart: 4, of which 3 were waited for; matrix products, arithmetic and copies ran while one was open for 7% of the time, Pallas kernels for 0%

commit v1 on v0

--- a/solution.py
+++ b/solution.py
@@ -64,7 +64,9 @@
     inner = jnp.einsum(
         "rd,mdu->mru",
         hidden,
-        lax.all_gather(medusa_w, "blk", axis=1, tiled=True),
+        jnp.concatenate(
+            lax.all_to_all(jnp.stack([medusa_w] * lax.axis_size("blk")), "blk", 0, 0), axis=1
+        ),
         preferred_element_type=jnp.float32,
     )
     own_cols = lax.dynamic_slice_in_dim(hidden, lax.axis_index("mp") * units, units, 1).astype(

time: 382 us -> 459 us (1.20)
  blocking collectives: 190 us -> 283 us
  waiting for transfers between devices: 99.3 us -> 64.8 us
  local copies, waits for them, and re-layouts: 27.5 us -> 42 us
  starting transfers between devices: 0.56 us -> 9.17 us
  matrix products: 43.3 us -> 38.7 us
    psum x1, blocking collectives: 125 us -> 218 us  [per_device(): summed = lax.psum((numer, denom), 'blk')]
    all_gather x1 -> x0, waiting for transfers between devices: 32.7 us -> none  [per_device(): lax.all_gather(medusa_w, 'blk', axis=1, tiled=True)]
    all_to_all x0 -> x1, starting transfers between devices: none -> 8.64 us  [per_device(): lax.all_to_all(jnp.stack([medusa_w] * lax.axis_size('blk')), 'blk', 0, 0)]
    another operation x0 -> x1, local copies, waits for them, and re-layouts: none -> 6.58 us  [per_device(): jnp.stack([medusa_w] * lax.axis_size('blk'))]
    reshape x0 -> x1, local copies, waits for them, and re-layouts: none -> 6.38 us  [per_device(): jnp.concatenate(lax.all_to_all(jnp.stack([medusa_w] * lax.axis_size('blk'...]
  transfers between devices with their start and end apart: 4 -> 4, of which waited for: 3 -> 2; matrix products, arithmetic and copies ran while one was open for 7% -> 15% of each run, Pallas kernels for 0% -> 0%
where the time goes in v1:
time: 459 us
  blocking collectives  283 us (62%)
  waiting for transfers between devices  64.8 us (14%)
  local copies, waits for them, and re-layouts  42 us (9%)
  matrix products  38.7 us (8%)
  between operations  16 us (3%)
  starting transfers between devices  9.17 us (2%)
  other arithmetic  5.25 us (1%)
    psum x1, blocking collectives, per_device(): summed = lax.psum((numer, denom), 'blk')  218 us
    psum x1, blocking collectives, per_device(): totals, picked = lax.psum((totals, picked), ('blk', 'mp'))  64.9 us
    psum x1, waiting for transfers between devices, per_device(): lax.psum(jnp.dot(heads_out, out_weight, preferred_element_type=jnp.float3...  32.9 us
    all_gather x1, waiting for transfers between devices, per_device(): full_fresh = lax.all_gather(fresh, 'mp', axis=2, tiled=True)  31.9 us
    dot_general x2, matrix products, attend(): jnp.einsum('qhrd,khd->hrqk', query_view, key_view, preferred_element_type...  12 us
    dot_general x2, matrix products, attend(): jnp.einsum('hrqk,khd->qhrd', weights.astype(jnp.bfloat16), value_view, pr...  9.63 us
  transfers between devices with their start and end apart: 4, of which 2 were waited for; matrix products, arithmetic and copies ran while one was open for 15% of the time, Pallas kernels for 0%

profile of v1, /device:TPU:1, one launch (start us, length us, event | category | flops | bytes accessed | tf_op | source)
XLA Modules:
  0.0 458.6 jit_solution(8715307443991996291)
XLA Ops:
  7.2 6.6 %stack.2 = bf16[32,2,112,896]{3,2,1,0:T(8,128)(2,1)} broadcast(bf16[2,112,896]{2,1,0:T(8,128)(2,1)} %param.15), dimensions={1,2,3} | broadcast | bytes 13246464 | tf_op jit(solution)/shard_map/stack | solution.py:68
  13.7 8.6 %all-to-all-start = ((bf16[32,2,112,896]{3,2,1,0:T(8,128)(2,1)}), bf16[32,2,112,896]{3,2,1,0:T(8,128)(2,1)}, u32[]{:S(2)}, u32[]{:S(2)}) async-start(bf16[32,2,112,896]{3,2,1,0:T(8,128)(2,1)} %stack.2), calls=%async_computation | async-start | bytes 25690112 | tf_op jit(solution)/shard_map/all_to_all | solution.py:68
  22.4 4.4 fusion.51
  26.9 2.9 copy.81
  31.7 3.3 reshape_reshape.3
  35.1 4.0 copy.82
  39.4 9.9 %fusion = (f32[2,2,576]{2,1,0:T(2,128)S(1)}, f32[2,2048,576,2]{1,2,3,0:T(8,128)}) fusion(f32[576,2048]{1,0:T(8,128)S(1)} %broadcast_multiply_fusion, bf16[2048,2,256,1]{0,2,3,1:T(8,128)(2,1)S(1)} %bitcast.86, bf16[576,2,2,256]{3,2,1,0:T(2,128)(2,1)S(1)} %reshape_reshape.3), kind=kOutput, calls=%fused_computation.1 | convolution fusion | flops 2434791168 | bytes 26878976 | tf_op jit(solution)/shard_map/qhrd,khd->hrqk/dot_general | solution.py:33
  49.3 9.1 %fusion.6 = f32[576,2,2,256]{3,0,2,1:T(8,128)S(1)} fusion(bf16[2048,2,256,1]{0,2,3,1:T(8,128)(2,1)S(1)} %bitcast.88, f32[2,2048,576,2]{1,2,3,0:T(8,128)} %get-tuple-element.15, f32[576,2048]{1,0:T(8,128)S(1)} %broadcast_multiply_fusion), kind=kOutput, calls=%fused_computation.10 | convolution fusion | flops 2434793472 | bytes 28049408 | tf_op jit(solution)/shard_map/hrqk,khd->qhrd/dot_general | solution.py:38
  58.4 1.8 copy.58
  60.3 2.9 reshape.111
  63.9 0.6 convolution_minimum_fusion.5
  64.5 0.4 convolution_minimum_fusion.4
  64.9 0.4 convolution_minimum_fusion.3
  65.3 0.4 convolution_minimum_fusion.2
  65.8 1.3 fusion.52
  67.5 1.7 reshape.112
  70.0 2.2 fusion.53
  72.2 217.7 %psum.38 = f32[576,4]{0,1:T(4,128)S(1)} all-reduce(f32[576,4]{0,1:T(4,128)S(1)} %reshape.114), channel_id=1, replica_groups=mesh['blk'=32,'mp'=4] {'blk'}, use_global_device_ids=true, to_apply=%region_6.7 | all-reduce | flops 2304 | bytes 18432 | tf_op jit(solution)/shard_map/psum | solution.py:101
  290.4 0.5 convolution_bitcast_fusion
  290.9 1.8 copy.64
  292.7 2.9 reshape.113
  295.8 5.1 %fusion.39 = f32[18,3584]{1,0:T(8,128)} fusion(bf16[1024,3584]{1,0:T(8,128)(2,1)} %param.25, f32[18,1024]{1,0:T(8,128)S(1)} %bitcast.90, f32[576,1024]{1,0:T(8,128)} %reshape.113, s32[]{:T(128)S(6)} %select_n.25, f32[576,1024]{1,0:T(8,128)} %all-reduce.4.cloned.1.call-done), kind=kOutput, calls=%fused_computation.47 | convolution fusion | flops 132175872 | bytes 7868420 | tf_op jit(solution)/shard_map/dot_general | solution.py:120
  301.1 6.4 %copy.52 = bf16[2,32,112,896]{3,2,1,0:T(8,128)(2,1)S(1)} copy(bf16[2,32,112,896]{3,2,0,1:T(8,128)(2,1)} %bitcast) | data formatting | bytes 25690112 | tf_op jit(solution)/shard_map/reshape | solution.py:67
  307.5 3.1 add_convert_fusion
  310.7 32.9 %all-reduce.6.cloned.1.call-done = f32[18,3584]{1,0:T(8,128)} async-done(((f32[18,3584]{1,0:T(8,128)}), f32[18,3584]{1,0:T(8,128)}) %all-reduce.6.cloned.1.call-update) | async-done | bytes 258064 | tf_op jit(solution)/shard_map/psum | solution.py:120
  343.6 1.1 multiply_reduce_fusion
  344.8 1.8 add_convert_fusion.1
  346.5 31.9 %all-gather.2.cloned.1.call-done = bf16[2,144,3584]{2,1,0:T(8,128)(2,1)} async-done(((bf16[2,144,896]{2,1,0:T(8,128)(2,1)}), bf16[2,144,3584]{2,1,0:T(8,128)(2,1)}) %all-gather.2.cloned.1.call-update) | async-done | bytes 2064400 | tf_op jit(solution)/shard_map/all_gather | solution.py:76
  378.4 6.2 %exponential_reduce_fusion = (f32[2,144]{1,0:T(2,128)S(1)}, f32[2,144,1024]{2,1,0:T(8,128)S(1)}) fusion(bf16[2,144,3584]{2,1,0:T(8,128)(2,1)} %all-gather.2.cloned.1.call-done, bf16[1024,3584]{1,0:T(8,128)(2,1)} %param.16), kind=kOutput, calls=%fused_computation.24 | convolution fusion | flops 2114813696 | bytes 10585216 | tf_op jit(solution)/shard_map/mrd,vd->mrv/dot_general | solution.py:78
  384.6 1.8 select_reduce_fusion
  386.5 64.9 %all-reduce = (f32[2,144,10]{1,2,0:T(8,128)S(1)}, f32[2,144]{1,0:T(2,128)S(1)}) all-reduce(f32[2,144,10]{1,2,0:T(8,128)S(1)} %select_reduce_fusion, f32[2,144]{1,0:T(2,128)S(1)} %get-tuple-element.10), channel_id=1, replica_groups=mesh['blk'=32,'mp'=4] {'blk','mp'}, use_global_device_ids=true, to_apply=%region_1.2 | all-reduce | flops 3168 | bytes 25344 | tf_op jit(solution)/shard_map/psum | solution.py:86
  451.4 0.6 copy.67
  (46 shorter events, 3.1 us)
Async XLA Ops:
  13.7 287.4 %all-to-all-start = ((bf16[32,2,112,896]{3,2,1,0:T(8,128)(2,1)}), bf16[32,2,112,896]{3,2,1,0:T(8,128)(2,1)}, u32[]{:S(2)}, u32[]{:S(2)}) async-start(bf16[32,2,112,896]{3,2,1,0:T(8,128)(2,1)} %stack.2), calls=%async_computation | async-start | bytes 25690112 | tf_op jit(solution)/shard_map/all_to_all | solution.py:68
  22.4 273.4 %all-reduce.4.cloned.1.call-start = ((), (), s32[]{:S(2)}) async-start(), calls=%async_computation.2 | async-start | bytes 4718592 | tf_op jit(solution)/shard_map/psum | solution.py:101
  39.4 9.9 %copy-start.1 = (bf16[1,1,2048,512]{2,3,1,0:T(8,128)(2,1)S(1)}, bf16[1,1,2048,512]{2,3,1,0:T(8,128)(2,1)}, u32[]{:S(2)}) copy-start(bf16[1,1,2048,512]{2,3,1,0:T(8,128)(2,1)} %copy.82) | copy-start | bytes 6291460
  63.2 0.7 copy-start.6
  63.2 280.4 %all-reduce.6.cloned.1.call-start = ((), (), s32[]{:S(2)}) async-start(), calls=%async_computation.3 | async-start | bytes 688128 | tf_op jit(solution)/shard_map/psum | solution.py:120
  64.9 2.6 copy-start
  292.7 3.0 copy-start.3
  300.8 77.5 %all-gather.2.cloned.1.call-start = ((), (), s32[]{:S(2)}) async-start(), calls=%async_computation.1 | async-start | bytes 2580480 | tf_op jit(solution)/shard_map/all_gather | solution.py:76
  307.5 3.2 copy-start.4
  307.5 37.2 %copy-start.2 = (bf16[18,3584]{1,0:T(8,128)(2,1)S(1)}, bf16[18,3584]{1,0:T(8,128)(2,1)}, u32[]{:S(2)}) copy-start(bf16[18,3584]{1,0:T(8,128)(2,1)} %param.27) | copy-start | bytes 387076
  307.5 37.2 %copy-start.5 = (f32[3584]{0:T(1024)S(1)}, f32[3584]{0:T(1024)}, u32[]{:S(2)}) copy-start(f32[3584]{0:T(1024)} %param.26) | copy-start | bytes 43012
Sparse Core Ops, SparseCore 0:
  63.3 209.1 all-reduce.3
  301.0 42.5 all-reduce.5
  345.3 33.0 all-gather.1
